TPU v7x, 512 devices: a whole 4x8x8 slice. The times are simulated.
512 devices in a mesh: pb: 32 (over z, x), ka: 16 (over y, core).
Axes of the slice: x: 4, y: 8, z: 8, core: 2. Of those that a mesh axis runs over, the one named last changes fastest.
Arguments:
- features: bfloat16 [65536, 1024], P(('pb', 'ka')), may hold values from -8.5 to 8.5
- order: int32 [65536], P(('pb', 'ka')), may hold values from 0 to 127, as said below
- neighbours: int32 [512, 24], P('pb'), may hold values from 0 to 511, as said below
- counts: int32 [512], P('pb'), may hold values from 1 to 24, as said below
- qkv_weight: bfloat16 [1024, 1536], P(('pb', 'ka')), may hold values from -0.25 to 0.25
- out_weight: bfloat16 [512, 1024], P(None, ('pb', 'ka')), may hold values from -1 to 1
Outputs:
- mixed: bfloat16 [65536, 1024], P(('pb', 'ka'))
Inputs may be any that keep to these rules, and one draw needn't show every extreme that they name: `order`: each aligned group of 128 entries is a permutation of 0 to 127. `neighbours`: entry 0 of the list of block a is a itself; the first counts[a] entries are distinct and lie in a's slab of 16 blocks or in the slabs just before and after it, cyclically; slots from counts[a] on hold some block id and are not part of the list. `counts`: some block's list fills all 24 slots.
All inputs are finite; a program needn't handle non-finite values.
Results may differ from a plain program's by a relative error of at most 0.012.
The roundings to bfloat16 on the way count: a program that leaves them out, or rounds other values in their place, can miss the bound.
Values may be sent and summed in bfloat16 or wider, within the bound.
No kernel may reach another device: no remote copies, remote signals or barrier semaphores. Data moves between devices by JAX's collectives and lax.ppermute only.
A program may use at most 64 MiB of HBM per device.

v0:
```python
import jax
import jax.numpy as jnp
from jax import lax
from jax.sharding import PartitionSpec as P

HD = 64
BLK = 128


def padded(array, sides, width):
    for axis, dim in sides:
        size, length = (lax.axis_size(axis), array.shape[dim])
        up = [(i, (i + 1) % size) for i in range(size)]
        down = [(j, i) for i, j in up]
        last = lax.slice_in_dim(array, length - width, length, axis=dim)
        leading = lax.slice_in_dim(array, 0, width, axis=dim)
        before = lax.ppermute(last, axis, up)
        after = lax.ppermute(leading, axis, down)
        array = jnp.concatenate([before, array, after], axis=dim)
    return array


def attend_rows(query_rows, allow_rows, near_keys, near_values, score_scale):
    row_total = query_rows.shape[0]
    head_count = query_rows.shape[1]
    attn_width = head_count * query_rows.shape[2]
    tile_rows = 512
    tile_count = row_total // tile_rows

    def attend(tile_args):
        query_tile, allow_tile = tile_args
        allowed = jnp.repeat(allow_tile, BLK, axis=1)
        scores = (
            jnp.einsum("qhd,khd->hqk", query_tile, near_keys, preferred_element_type=jnp.float32)
            * score_scale
        )
        row_max = jnp.max(jnp.where(allowed[None], scores, -1e30), axis=-1)
        row_shift = row_max.astype(jnp.bfloat16)
        soft_weights = jnp.where(
            allowed[None], jnp.exp(scores - row_shift.astype(jnp.float32)[..., None]), 0.0
        )
        group_total = jnp.sum(soft_weights, axis=-1).T
        numerator = jnp.einsum(
            "hqk,khd->qhd",
            soft_weights.astype(jnp.bfloat16),
            near_values,
            preferred_element_type=jnp.float32,
        )
        positive = group_total > 0
        partial_value = jnp.where(
            positive[..., None], numerator / jnp.where(positive, group_total, 1.0)[..., None], 0.0
        )
        return (
            partial_value.astype(jnp.bfloat16).reshape(tile_rows, attn_width),
            row_shift.T,
            group_total.astype(jnp.bfloat16),
        )

    tiled = lax.map(
        attend,
        (
            query_rows.reshape(tile_count, tile_rows, head_count, query_rows.shape[2]),
            allow_rows.reshape(tile_count, tile_rows, -1),
        ),
    )
    return (
        tiled[0].reshape(row_total, attn_width),
        tiled[1].reshape(row_total, head_count),
        tiled[2].reshape(row_total, head_count),
    )


def body(features, order, neighbours, counts, qkv_weight, out_weight):
    dev_rows = features.shape[0]
    sorted_rows = jnp.take(features, order, axis=0)
    attn_width = qkv_weight.shape[1] // 3
    head_count = attn_width // HD
    score_scale = HD ** (-0.5)
    projected = jnp.dot(
        sorted_rows,
        lax.all_gather(qkv_weight, ("pb", "ka"), axis=0, tiled=True),
        preferred_element_type=jnp.float32,
    )
    own_queries = projected[:, :attn_width].astype(jnp.bfloat16)
    keys_values = projected[:, attn_width:].astype(jnp.bfloat16)
    near = padded(keys_values, (("pb", 0),), dev_rows)
    slab_index = lax.axis_index("pb")
    group_index = lax.axis_index("ka")
    slab_count = lax.axis_size("pb")
    group_count = lax.axis_size("ka")
    dev_blocks = dev_rows // BLK
    slab_of = (slab_index + jnp.arange(3) - 1) % slab_count
    listed_slot = jnp.arange(neighbours.shape[1])[None, :] < counts[:, None]
    slab_queries = lax.all_gather(own_queries, "ka", axis=0, tiled=True)
    near_keys = near[:, :attn_width].reshape(3 * dev_rows, head_count, HD)
    near_values = near[:, attn_width:].reshape(3 * dev_rows, head_count, HD)
    block_ids = (
        (slab_of[:, None] * group_count + group_index) * dev_blocks
        + jnp.arange(dev_blocks)[None, :]
    ).reshape(-1)
    member = jnp.any(
        (neighbours[:, :, None] == block_ids[None, None, :]) & listed_slot[:, :, None], axis=1
    )
    row_member = jnp.repeat(member, BLK, axis=0)
    partial_value, row_shift, group_total = attend_rows(
        slab_queries.reshape(-1, head_count, HD), row_member, near_keys, near_values, score_scale
    )
    received = (
        lax.all_to_all(partial_value[None], "ka", split_axis=1, concat_axis=0, tiled=True),
        lax.all_to_all(row_shift[None], "ka", split_axis=1, concat_axis=0, tiled=True),
        lax.all_to_all(group_total[None], "ka", split_axis=1, concat_axis=0, tiled=True),
    )
    group_out = received[0].reshape(group_count, dev_rows, head_count, HD).astype(jnp.float32)
    group_max = received[1].astype(jnp.float32)
    total_rounded = received[2].astype(jnp.float32)
    top_shift = jnp.max(group_max, axis=0, keepdims=True)
    weight_g = total_rounded * jnp.exp(group_max - top_shift)
    combined = (
        jnp.sum(weight_g[..., None] * group_out, axis=0) / jnp.sum(weight_g, axis=0)[..., None]
    )
    attended = combined.reshape(dev_rows, attn_width).astype(jnp.bfloat16)
    mixed = jnp.dot(
        attended,
        lax.all_gather(out_weight, ("pb", "ka"), axis=1, tiled=True),
        preferred_element_type=jnp.float32,
    )
    return mixed.astype(jnp.bfloat16)


def solution(mesh):
    return jax.shard_map(
        body,
        mesh=mesh,
        in_specs=(
            P(("pb", "ka"), None),
            P(("pb", "ka")),
            P("pb", None),
            P("pb"),
            P(("pb", "ka"), None),
            P(None, ("pb", "ka")),
        ),
        out_specs=P(("pb", "ka"), None),
        check_vma=False,
    )
```

profile of v0, /device:TPU:1, one launch (start us, length us, event | category | flops | bytes accessed | tf_op | source)
XLA Modules:
  0.0 470.9 jit_solution(14192227212871008691)
XLA Ops:
  10.2 124.0 %all-gather.8.cloned.1.call-done = bf16[512,2,1536]{2,1,0:T(2,128)(2,1)} async-done(((bf16[1,2,1536]{2,1,0:T(2,128)(2,1)}), bf16[512,2,1536]{2,1,0:T(2,128)(2,1)}) %all-gather.8.cloned.1.call-update) | async-done | bytes 3145744 | tf_op jit(solution)/shard_map/all_gather | solution.py:81
  134.2 6.3 %reshape.136 = bf16[1024,1536]{1,0:T(8,128)(2,1)S(1)} reshape(bf16[512,2,1536]{2,1,0:T(2,128)(2,1)} %all-gather.8.cloned.1.call-done) | data formatting | bytes 6291456
  144.6 3.1 collective-permute-start
  147.6 5.7 %collective-permute-start.1 = (bf16[128,1024]{1,0:T(8,128)(2,1)S(1)}, bf16[128,1024]{1,0:T(8,128)(2,1)S(1)}, u32[]{:S(2)}, u32[]{:S(2)}) collective-permute-start(bf16[128,1024]{1,0:T(8,128)(2,1)S(1)} %slice.21), channel_id=1, source_target_pairs={{16,0},{32,16},{48,32},{64,48},{80,64},{96,80},{112,96},{128,112},... | collective-permute-start | bytes 786440 | tf_op jit(solution)/shard_map/ppermute | solution.py:18
  153.8 3.6 collective-permute-done
  158.8 22.9 %all-gather.6.cloned.1.call-done = bf16[2048,512]{1,0:T(8,128)(2,1)} async-done(((bf16[128,512]{1,0:T(8,128)(2,1)}), bf16[2048,512]{1,0:T(8,128)(2,1)}) %all-gather.6.cloned.1.call-update) | async-done | bytes 2097168 | tf_op jit(solution)/shard_map/all_gather | solution.py:94
  181.7 6.2 %reshape.139 = bf16[4,512,8,64]{3,2,1,0:T(8,128)(2,1)} reshape(bf16[2048,512]{1,0:T(8,128)(2,1)} %all-gather.6.cloned.1.call-done) | data formatting | bytes 4194304 | tf_op jit(solution)/shard_map/reshape;reshape | solution.py:62
  187.9 5.5 %copy.79 = bf16[4,512,8,64]{1,3,2,0:T(8,128)(2,1)} copy(bf16[4,512,8,64]{3,2,1,0:T(8,128)(2,1)} %reshape.139) | data formatting | bytes 4194304 | tf_op jit(solution)/shard_map/while | solution.py:59
  193.3 24.9 %while.14 = (s32[]{:T(128)}, bf16[4,512,512]{2,1,0:T(8,128)(2,1)}, bf16[4,512,8]{1,2,0:T(8,128)(2,1)S(1)}, bf16[4,512,8]{1,2,0:T(8,128)(2,1)S(1)}, pred[4,512,3]...) while((s32[]{:T(128)}, bf16[4,512,512]{2,1,0:T(8,128)(2,1)}, ...), condition=%wide.region_4.5_spmd, body=%wide.region_1.4_spmd.sunk | while | flops 420753408 | bytes 23795300 | solution.py:59
  219.4 12.2 %reduce.6 = bf16[2048,8]{1,0:T(8,128)(2,1)} reduce(bf16[2048,1,8]{2,1,0:T(2,128)(2,1)S(1)} %bitcast.101, bf16[]{:T(256)} %broadcast.127), dimensions={1}, to_apply=%bitcast.57.reduce_sub_computation | reduce | bytes 65538
  233.8 4.9 %all-to-all-start.1 = ((bf16[16,2,512]{2,1,0:T(2,128)(2,1)}), bf16[16,2,512]{2,1,0:T(2,128)(2,1)S(1)}, u32[]{:S(2)}, u32[]{:S(2)}) async-start(bf16[16,2,512]{2,1,0:T(2,128)(2,1)} %reshape.144), calls=%async_computation.1 | async-start | bytes 65536 | tf_op jit(solution)/shard_map/all_to_all | solution.py:110
  239.5 12.2 %reduce.7 = bf16[2048,8]{1,0:T(8,128)(2,1)} reduce(bf16[2048,1,8]{2,1,0:T(2,128)(2,1)S(1)} %bitcast.102, bf16[]{:T(256)} %broadcast.127), dimensions={1}, to_apply=%bitcast.55.reduce_sub_computation | reduce | bytes 65538
  253.9 7.2 %all-to-all-start = ((bf16[16,2,512]{2,1,0:T(2,128)(2,1)}), bf16[16,2,512]{2,1,0:T(2,128)(2,1)S(1)}, u32[]{:S(2)}, u32[]{:S(2)}) async-start(bf16[16,2,512]{2,1,0:T(2,128)(2,1)} %reshape.142), calls=%async_computation | async-start | bytes 65536 | tf_op jit(solution)/shard_map/all_to_all | solution.py:111
  261.1 18.5 %copy.97 = bf16[1,2048,512]{2,0,1:T(2,128)(2,1)} copy(bf16[1,2048,512]{2,1,0:T(8,128)(2,1)S(1)} %bitcast.105) | data formatting | bytes 4194304 | tf_op jit(solution)/shard_map/broadcast_in_dim;reshape | solution.py:109
  279.7 14.0 %reduce.5 = bf16[2048,512]{1,0:T(8,128)(2,1)S(1)} reduce(bf16[2048,1,512]{2,1,0:T(2,128)(2,1)} %bitcast.95, bf16[]{:T(256)} %broadcast.127), dimensions={1}, to_apply=%bitcast.69.reduce_sub_computation | reduce | bytes 4194306
  293.7 2.8 reshape.140
  296.5 7.2 %all-to-all-start.2 = ((bf16[16,2,32768]{2,1,0:T(2,128)(2,1)}), bf16[16,2,32768]{2,1,0:T(2,128)(2,1)S(1)}, u32[]{:S(2)}, u32[]{:S(2)}) async-start(bf16[16,2,32768]{2,1,0:T(2,128)(2,1)} %reshape.140), calls=%async_computation.2 | async-start | bytes 4194304 | tf_op jit(solution)/shard_map/all_to_all | solution.py:109
  304.4 126.7 %all-gather.10.cloned.1.call-done = bf16[512,2,512]{2,1,0:T(2,128)(2,1)} async-done(((bf16[1,2,512]{2,1,0:T(2,128)(2,1)}), bf16[512,2,512]{2,1,0:T(2,128)(2,1)}) %all-gather.10.cloned.1.call-update) | async-done | bytes 1048592 | tf_op jit(solution)/shard_map/all_gather | solution.py:124
  432.6 2.5 reshape.145
  437.4 2.5 reshape.143
  442.2 6.8 %reshape.141 = bf16[2048,1,512]{2,1,0:T(2,128)(2,1)} reshape(bf16[16,2,32768]{2,1,0:T(2,128)(2,1)S(1)} %all-to-all-done.2) | data formatting | bytes 4194304
  449.0 4.6 copy_convert_fusion
  453.6 5.5 %copy.88 = f32[1,2048,512]{1,2,0:T(8,128)} copy(f32[1,2048,512]{2,1,0:T(8,128)} %copy_convert_fusion) | data formatting | bytes 8388608 | tf_op jit(solution)/shard_map/convert_element_type | solution.py:113
  459.1 3.1 copy.94
  (99 shorter events, 49.2 us)
Async XLA Ops:
  6.5 1.4 copy-start
  6.5 127.7 %all-gather.8.cloned.1.call-start = ((), (), s32[]{:S(2)}) async-start(), calls=%async_computation.4 | async-start | bytes 3151872 | tf_op jit(solution)/shard_map/all_gather | solution.py:81
  7.3 174.4 %all-gather.6.cloned.1.call-start = ((), (), s32[]{:S(2)}) async-start(), calls=%async_computation.3 | async-start | bytes 2228224 | tf_op jit(solution)/shard_map/all_gather | solution.py:94
  10.2 143.2 %copy-start.4 = (s32[16]{0:T(128)S(1)}, s32[16]{0:T(128)}, u32[]{:S(2)}) copy-start(s32[16]{0:T(128)} %param.11) | copy-start | bytes 196
  10.2 143.3 %copy-start.3 = (s32[16,24]{1,0:T(8,128)S(1)}, s32[16,24]{1,0:T(8,128)}, u32[]{:S(2)}) copy-start(s32[16,24]{1,0:T(8,128)} %param.10) | copy-start | bytes 4612
  142.2 0.7 copy-start.2
  144.6 12.8 %collective-permute-start = (bf16[128,1024]{1,0:T(8,128)(2,1)S(1)}, bf16[128,1024]{1,0:T(8,128)(2,1)S(1)}, u32[]{:S(2)}, u32[]{:S(2)}) collective-permute-start(bf16[128,1024]{1,0:T(8,128)(2,1)S(1)} %slice.21), channel_id=1, source_target_pairs={{0,16},{16,32},{32,48},{48,64},{64,80},{80,96},{96,112},{112,128},... | collective-permute-start | bytes 786440 | tf_op jit(solution)/shard_map/ppermute | solution.py:17
  147.6 10.6 %collective-permute-start.1 = (bf16[128,1024]{1,0:T(8,128)(2,1)S(1)}, bf16[128,1024]{1,0:T(8,128)(2,1)S(1)}, u32[]{:S(2)}, u32[]{:S(2)}) collective-permute-start(bf16[128,1024]{1,0:T(8,128)(2,1)S(1)} %slice.21), channel_id=1, source_target_pairs={{16,0},{32,16},{48,32},{64,48},{80,64},{96,80},{112,96},{128,112},... | collective-permute-start | bytes 786440 | tf_op jit(solution)/shard_map/ppermute | solution.py:18
  218.2 42.9 %copy-start.1 = (bf16[4,512,512]{2,1,0:T(8,128)(2,1)S(1)}, bf16[4,512,512]{2,1,0:T(8,128)(2,1)}, u32[]{:S(2)}) copy-start(bf16[4,512,512]{2,1,0:T(8,128)(2,1)} %get-tuple-element.51) | copy-start | bytes 6291460
  233.8 20.1 %all-to-all-start.1 = ((bf16[16,2,512]{2,1,0:T(2,128)(2,1)}), bf16[16,2,512]{2,1,0:T(2,128)(2,1)S(1)}, u32[]{:S(2)}, u32[]{:S(2)}) async-start(bf16[16,2,512]{2,1,0:T(2,128)(2,1)} %reshape.144), calls=%async_computation.1 | async-start | bytes 65536 | tf_op jit(solution)/shard_map/all_to_all | solution.py:110
  253.9 42.6 %all-to-all-start = ((bf16[16,2,512]{2,1,0:T(2,128)(2,1)}), bf16[16,2,512]{2,1,0:T(2,128)(2,1)S(1)}, u32[]{:S(2)}, u32[]{:S(2)}) async-start(bf16[16,2,512]{2,1,0:T(2,128)(2,1)} %reshape.142), calls=%async_computation | async-start | bytes 65536 | tf_op jit(solution)/shard_map/all_to_all | solution.py:111
  296.5 145.7 %all-to-all-start.2 = ((bf16[16,2,32768]{2,1,0:T(2,128)(2,1)}), bf16[16,2,32768]{2,1,0:T(2,128)(2,1)S(1)}, u32[]{:S(2)}, u32[]{:S(2)}) async-start(bf16[16,2,32768]{2,1,0:T(2,128)(2,1)} %reshape.140), calls=%async_computation.2 | async-start | bytes 4194304 | tf_op jit(solution)/shard_map/all_to_all | solution.py:109
  303.7 127.5 %all-gather.10.cloned.1.call-start = ((), (), s32[]{:S(2)}) async-start(), calls=%async_computation.5 | async-start | bytes 1050624 | tf_op jit(solution)/shard_map/all_gather | solution.py:124
Sparse Core Ops, SparseCore 0:
  11.5 122.6 all-gather.7
  143.7 37.9 all-gather.5
  308.7 122.4 all-gather.9
where the time goes:
time: 472 us; the launch traced here: 471 us
  waiting for transfers between devices  279 us (59%)
  local copies, waits for them, and re-layouts  80.9 us (17%)
  other arithmetic  51.1 us (11%)
  starting transfers between devices  28.5 us (6%)
  matrix products  17.6 us (4%)
  between operations  13.3 us (3%)
    all_gather x1, waiting for transfers between devices, body(): lax.all_gather(out_weight, ('pb', 'ka'), axis=1, tiled=True)  127 us
    all_gather x1, waiting for transfers between devices, body(): lax.all_gather(qkv_weight, ('pb', 'ka'), axis=0, tiled=True)  124 us
    unnamed x3, other arithmetic  38.5 us
    unnamed x20, local copies, waits for them, and re-layouts  31.1 us
    all_gather x1, waiting for transfers between devices, body(): slab_queries = lax.all_gather(own_queries, 'ka', axis=0, tiled=True)  22.9 us
    another operation x1, local copies, waits for them, and re-layouts, body(): partial_value[None]  18.5 us
  transfers between devices with their start and end apart: 8, of which 5 were waited for; matrix products, arithmetic and copies ran while one was open for 14% of the time, Pallas kernels for 0%

commit v1 on v0

--- a/solution.py
+++ b/solution.py
@@ -91,7 +91,9 @@
     dev_blocks = dev_rows // BLK
     slab_of = (slab_index + jnp.arange(3) - 1) % slab_count
     listed_slot = jnp.arange(neighbours.shape[1])[None, :] < counts[:, None]
-    slab_queries = lax.all_gather(own_queries, "ka", axis=0, tiled=True)
+    slab_queries = jnp.concatenate(
+        lax.all_to_all(jnp.stack([own_queries] * lax.axis_size("ka")), "ka", 0, 0), axis=0
+    )
     near_keys = near[:, :attn_width].reshape(3 * dev_rows, head_count, HD)
     near_values = near[:, attn_width:].reshape(3 * dev_rows, head_count, HD)
     block_ids = (

time: 472 us -> 489 us (1.036)
  waiting for transfers between devices: 279 us -> 289 us
    all_to_all x0 -> x1, waiting for transfers between devices: none -> 32 us  [body(): lax.all_to_all(jnp.stack([own_queries] * lax.axis_size('ka')), 'ka', 0, 0)]
    all_gather x1 -> x0, waiting for transfers between devices: 22.9 us -> none  [body(): slab_queries = lax.all_gather(own_queries, 'ka', axis=0, tiled=True)]
    unnamed x20 -> x22, local copies, waits for them, and re-layouts: 31.1 us -> 31.1 us
where the time goes in v1:
time: 489 us; the launch traced here: 488 us
  waiting for transfers between devices  289 us (59%)
  local copies, waits for them, and re-layouts  79.3 us (16%)
  other arithmetic  51.1 us (10%)
  starting transfers between devices  32.5 us (7%)
  matrix products  21.8 us (4%)
  between operations  13.6 us (3%)
    all_gather x1, waiting for transfers between devices, body(): lax.all_gather(out_weight, ('pb', 'ka'), axis=1, tiled=True)  127 us
    all_gather x1, waiting for transfers between devices, body(): lax.all_gather(qkv_weight, ('pb', 'ka'), axis=0, tiled=True)  124 us
    unnamed x3, other arithmetic  38.5 us
    all_to_all x1, waiting for transfers between devices, body(): lax.all_to_all(jnp.stack([own_queries] * lax.axis_size('ka')), 'ka', 0, 0)  32 us
    unnamed x22, local copies, waits for them, and re-layouts  31.1 us
    another operation x1, local copies, waits for them, and re-layouts, body(): partial_value[None]  18.5 us
    dot_general x4, matrix products, attend(): jnp.einsum('hqk,khd->qhd', soft_weights.astype(jnp.bfloat16), near_values...  10.2 us
  transfers between devices with their start and end apart: 8, of which 5 were waited for; matrix products, arithmetic and copies ran while one was open for 14% of the time, Pallas kernels for 0%

profile of v1, /device:TPU:1, one launch (start us, length us, event | category | flops | bytes accessed | tf_op | source)
XLA Modules:
  0.0 487.7 jit_solution(14466848398246503076)
XLA Ops:
  10.2 124.1 %all-gather.5.cloned.1.call-done = bf16[512,2,1536]{2,1,0:T(2,128)(2,1)} async-done(((bf16[1,2,1536]{2,1,0:T(2,128)(2,1)}), bf16[512,2,1536]{2,1,0:T(2,128)(2,1)}) %all-gather.5.cloned.1.call-update) | async-done | bytes 3145744 | tf_op jit(solution)/shard_map/all_gather | solution.py:81
  134.2 6.3 %reshape.138 = bf16[1024,1536]{1,0:T(8,128)(2,1)S(1)} reshape(bf16[512,2,1536]{2,1,0:T(2,128)(2,1)} %all-gather.5.cloned.1.call-done) | data formatting | bytes 6291456
  144.8 4.4 all-to-all-start
  149.3 2.8 collective-permute-start
  152.1 5.9 %collective-permute-start.1 = (bf16[128,1024]{1,0:T(8,128)(2,1)S(1)}, bf16[128,1024]{1,0:T(8,128)(2,1)S(1)}, u32[]{:S(2)}, u32[]{:S(2)}) collective-permute-start(bf16[128,1024]{1,0:T(8,128)(2,1)S(1)} %slice.21), channel_id=1, source_target_pairs={{16,0},{32,16},{48,32},{64,48},{80,64},{96,80},{112,96},{128,112},... | collective-permute-start | bytes 786440 | tf_op jit(solution)/shard_map/ppermute | solution.py:18
  158.4 4.0 collective-permute-done
  166.2 32.0 %all-to-all-done = bf16[16,128,512]{1,2,0:T(8,128)(2,1)S(1)} async-done(((bf16[16,128,512]{1,2,0:T(8,128)(2,1)}), bf16[16,128,512]{1,2,0:T(8,128)(2,1)S(1)}, u32[]{:S(2)}, u32[]{:S(2)}) %all-to-all-start) | async-done | bytes 2097184 | tf_op jit(solution)/shard_map/all_to_all | solution.py:95
  198.2 2.7 copy.79
  200.9 2.7 reshape_reshape_reshape.3
  205.5 29.0 %while.14 = (s32[]{:T(128)}, bf16[4,512,512]{2,1,0:T(8,128)(2,1)}, bf16[4,512,8]{1,2,0:T(8,128)(2,1)S(1)}, bf16[4,512,8]{1,2,0:T(8,128)(2,1)S(1)}, pred[4,512,3]...) while((s32[]{:T(128)}, bf16[4,512,512]{2,1,0:T(8,128)(2,1)}, ...), condition=%wide.region_4.5_spmd, body=%wide.region_1.4_spmd.sunk | while | flops 420753408 | bytes 23795300 | solution.py:59
  209.1 2.5 select_convert_fusion.2
  235.7 12.2 %reduce.6 = bf16[2048,8]{1,0:T(8,128)(2,1)} reduce(bf16[2048,1,8]{2,1,0:T(2,128)(2,1)S(1)} %bitcast.103, bf16[]{:T(256)} %broadcast.129), dimensions={1}, to_apply=%bitcast.59.reduce_sub_computation | reduce | bytes 65538
  250.1 5.0 %all-to-all-start.2 = ((bf16[16,2,512]{2,1,0:T(2,128)(2,1)}), bf16[16,2,512]{2,1,0:T(2,128)(2,1)S(1)}, u32[]{:S(2)}, u32[]{:S(2)}) async-start(bf16[16,2,512]{2,1,0:T(2,128)(2,1)} %reshape.145), calls=%async_computation.2 | async-start | bytes 65536 | tf_op jit(solution)/shard_map/all_to_all | solution.py:112
  255.8 12.2 %reduce.7 = bf16[2048,8]{1,0:T(8,128)(2,1)} reduce(bf16[2048,1,8]{2,1,0:T(2,128)(2,1)S(1)} %bitcast.104, bf16[]{:T(256)} %broadcast.129), dimensions={1}, to_apply=%bitcast.57.reduce_sub_computation | reduce | bytes 65538
  270.3 7.2 %all-to-all-start.1 = ((bf16[16,2,512]{2,1,0:T(2,128)(2,1)}), bf16[16,2,512]{2,1,0:T(2,128)(2,1)S(1)}, u32[]{:S(2)}, u32[]{:S(2)}) async-start(bf16[16,2,512]{2,1,0:T(2,128)(2,1)} %reshape.143), calls=%async_computation.1 | async-start | bytes 65536 | tf_op jit(solution)/shard_map/all_to_all | solution.py:113
  277.5 18.5 %copy.99 = bf16[1,2048,512]{2,0,1:T(2,128)(2,1)} copy(bf16[1,2048,512]{2,1,0:T(8,128)(2,1)S(1)} %bitcast.107) | data formatting | bytes 4194304 | tf_op jit(solution)/shard_map/broadcast_in_dim;reshape | solution.py:111
  296.0 14.0 %reduce.5 = bf16[2048,512]{1,0:T(8,128)(2,1)S(1)} reduce(bf16[2048,1,512]{2,1,0:T(2,128)(2,1)} %bitcast.97, bf16[]{:T(256)} %broadcast.129), dimensions={1}, to_apply=%bitcast.71.reduce_sub_computation | reduce | bytes 4194306
  310.0 2.8 reshape.141
  312.8 7.2 %all-to-all-start.3 = ((bf16[16,2,32768]{2,1,0:T(2,128)(2,1)}), bf16[16,2,32768]{2,1,0:T(2,128)(2,1)S(1)}, u32[]{:S(2)}, u32[]{:S(2)}) async-start(bf16[16,2,32768]{2,1,0:T(2,128)(2,1)} %reshape.141), calls=%async_computation.3 | async-start | bytes 4194304 | tf_op jit(solution)/shard_map/all_to_all | solution.py:111
  320.8 126.8 %all-gather.7.cloned.1.call-done = bf16[512,2,512]{2,1,0:T(2,128)(2,1)} async-done(((bf16[1,2,512]{2,1,0:T(2,128)(2,1)}), bf16[512,2,512]{2,1,0:T(2,128)(2,1)}) %all-gather.7.cloned.1.call-update) | async-done | bytes 1048592 | tf_op jit(solution)/shard_map/all_gather | solution.py:126
  458.7 6.8 %reshape.142 = bf16[2048,1,512]{2,1,0:T(2,128)(2,1)} reshape(bf16[16,2,32768]{2,1,0:T(2,128)(2,1)S(1)} %all-to-all-done.3) | data formatting | bytes 4194304
  465.5 4.6 copy_convert_fusion
  470.1 5.5 %copy.92 = f32[1,2048,512]{1,2,0:T(8,128)} copy(f32[1,2048,512]{2,1,0:T(8,128)} %copy_convert_fusion) | data formatting | bytes 8388608 | tf_op jit(solution)/shard_map/convert_element_type | solution.py:115
  475.6 3.1 copy.96
  (103 shorter events, 60.4 us)
Async XLA Ops:
  6.5 1.4 copy-start
  6.5 127.7 %all-gather.5.cloned.1.call-start = ((), (), s32[]{:S(2)}) async-start(), calls=%async_computation.4 | async-start | bytes 3151872 | tf_op jit(solution)/shard_map/all_gather | solution.py:81
  142.2 0.8 copy-start.2
  142.9 15.0 %copy-start.5 = (s32[16]{0:T(128)S(1)}, s32[16]{0:T(128)}, u32[]{:S(2)}) copy-start(s32[16]{0:T(128)} %param.11) | copy-start | bytes 196
  142.9 15.1 %copy-start.4 = (s32[16,24]{1,0:T(8,128)S(1)}, s32[16,24]{1,0:T(8,128)}, u32[]{:S(2)}) copy-start(s32[16,24]{1,0:T(8,128)} %param.10) | copy-start | bytes 4612
  142.9 6.3 %copy-start.3 = (bf16[128,1536]{1,0:T(8,128)(2,1)S(1)}, bf16[128,1536]{1,0:T(8,128)(2,1)}, u32[]{:S(2)}) copy-start(bf16[128,1536]{1,0:T(8,128)(2,1)} %copy-done.2) | copy-start | bytes 1179652
  144.8 53.4 %all-to-all-start = ((bf16[16,128,512]{1,2,0:T(8,128)(2,1)}), bf16[16,128,512]{1,2,0:T(8,128)(2,1)S(1)}, u32[]{:S(2)}, u32[]{:S(2)}) async-start(bf16[16,128,512]{1,2,0:T(8,128)(2,1)} %stack.2), calls=%async_computation | async-start | bytes 4194304 | tf_op jit(solution)/shard_map/all_to_all | solution.py:95
  149.3 13.1 %collective-permute-start = (bf16[128,1024]{1,0:T(8,128)(2,1)S(1)}, bf16[128,1024]{1,0:T(8,128)(2,1)S(1)}, u32[]{:S(2)}, u32[]{:S(2)}) collective-permute-start(bf16[128,1024]{1,0:T(8,128)(2,1)S(1)} %slice.21), channel_id=1, source_target_pairs={{0,16},{16,32},{32,48},{48,64},{64,80},{80,96},{96,112},{112,128},... | collective-permute-start | bytes 786440 | tf_op jit(solution)/shard_map/ppermute | solution.py:17
  152.1 11.2 %collective-permute-start.1 = (bf16[128,1024]{1,0:T(8,128)(2,1)S(1)}, bf16[128,1024]{1,0:T(8,128)(2,1)S(1)}, u32[]{:S(2)}, u32[]{:S(2)}) collective-permute-start(bf16[128,1024]{1,0:T(8,128)(2,1)S(1)} %slice.21), channel_id=1, source_target_pairs={{16,0},{32,16},{48,32},{64,48},{80,64},{96,80},{112,96},{128,112},... | collective-permute-start | bytes 786440 | tf_op jit(solution)/shard_map/ppermute | solution.py:18
  234.5 43.0 %copy-start.1 = (bf16[4,512,512]{2,1,0:T(8,128)(2,1)S(1)}, bf16[4,512,512]{2,1,0:T(8,128)(2,1)}, u32[]{:S(2)}) copy-start(bf16[4,512,512]{2,1,0:T(8,128)(2,1)} %get-tuple-element.51) | copy-start | bytes 6291460
  250.1 20.1 %all-to-all-start.2 = ((bf16[16,2,512]{2,1,0:T(2,128)(2,1)}), bf16[16,2,512]{2,1,0:T(2,128)(2,1)S(1)}, u32[]{:S(2)}, u32[]{:S(2)}) async-start(bf16[16,2,512]{2,1,0:T(2,128)(2,1)} %reshape.145), calls=%async_computation.2 | async-start | bytes 65536 | tf_op jit(solution)/shard_map/all_to_all | solution.py:112
  270.3 42.6 %all-to-all-start.1 = ((bf16[16,2,512]{2,1,0:T(2,128)(2,1)}), bf16[16,2,512]{2,1,0:T(2,128)(2,1)S(1)}, u32[]{:S(2)}, u32[]{:S(2)}) async-start(bf16[16,2,512]{2,1,0:T(2,128)(2,1)} %reshape.143), calls=%async_computation.1 | async-start | bytes 65536 | tf_op jit(solution)/shard_map/all_to_all | solution.py:113
  312.8 145.8 %all-to-all-start.3 = ((bf16[16,2,32768]{2,1,0:T(2,128)(2,1)}), bf16[16,2,32768]{2,1,0:T(2,128)(2,1)S(1)}, u32[]{:S(2)}, u32[]{:S(2)}) async-start(bf16[16,2,32768]{2,1,0:T(2,128)(2,1)} %reshape.141), calls=%async_computation.3 | async-start | bytes 4194304 | tf_op jit(solution)/shard_map/all_to_all | solution.py:111
  320.1 127.6 %all-gather.7.cloned.1.call-start = ((), (), s32[]{:S(2)}) async-start(), calls=%async_computation.5 | async-start | bytes 1050624 | tf_op jit(solution)/shard_map/all_gather | solution.py:126
Sparse Core Ops, SparseCore 0:
  11.5 122.6 all-gather.4
  325.1 122.5 all-gather.6
